TPU v7x, 768 devices: a whole 4x8x12 slice. The times are simulated.
768 devices in a mesh: wide: 64 (over y, x, core), narrow: 12 (over z).
Axes of the slice: x: 4, y: 8, z: 12, core: 2. Of those that a mesh axis runs over, the one named last changes fastest.
Arguments:
- momentum: bfloat16 [28672, 6144], P('wide', 'narrow'), may hold values from -60 to 60
- gradient: bfloat16 [28672, 6144], P('wide', 'narrow'), may hold values from -6 to 6
- right_prev: float32 [6144, 512], P('narrow'), may hold values from -0.078125 to 0.078125
Outputs:
- momentum_next: bfloat16 [28672, 6144], P('wide', 'narrow')
- weight_update: float32 [28672, 6144], P('wide', 'narrow')
- right_next: float32 [6144, 512], P('narrow')
All inputs are finite; a program needn't handle non-finite values.
Results may differ from a plain program's by a relative error of at most 0.009.
Values sent between devices are 32-bit elements; how exact they have to be, the bound alone decides.
A program may use at most 32 MiB of HBM per device.

v0:
```python
import math

import jax
import jax.numpy as jnp
from jax import lax
from jax.sharding import Mesh
from jax.sharding import PartitionSpec as P

FF = 28672
D = 6144
RANK = 512
WIDE = ("wide_0", "wide_1", "wide_2")
WIDE_NARROW = ("wide_0", "wide_1", "wide_2", "narrow")


def padded_to(lines, count):
    spare = -len(lines) % count
    return jnp.pad(lines, [(0, spare)] + [(0, 0)] * (lines.ndim - 1))


def sum_by_parts(shard, axis):
    lines = shard.reshape(-1, *shard.shape[1:][-1:])
    padded = padded_to(lines, lax.axis_size(axis))
    own = lax.psum_scatter(padded, axis, scatter_dimension=0, tiled=True)
    whole = lax.all_gather(own, axis, axis=0, tiled=True)
    return whole[: len(lines)].reshape(shard.shape)


def sum_in_order(parts, axes, turns):
    inside = parts.shape[1:]
    parts = parts.reshape(*(lax.axis_size(a) for a in axes), *inside)
    parts = jnp.moveaxis(parts, turns, range(len(axes))).reshape(-1, *inside)
    for k in turns:
        parts = lax.psum_scatter(parts, axes[k], scatter_dimension=0, tiled=True)
    return parts[0]


def gather_in_order(shard, axes, turns):
    parts = shard[None]
    for k in turns:
        parts = lax.all_gather(parts, axes[k], axis=0, tiled=True)
    current = [lax.axis_size(axes[k]) for k in reversed(turns)]
    parts = parts.reshape(*current, *shard.shape)
    turned = sorted(range(len(turns)), key=lambda place: turns[len(turns) - 1 - place])
    return parts.transpose(*turned, *range(len(turns), parts.ndim)).reshape(-1, *shard.shape)


def sum_in_two_steps(shard, axes, turns):
    count, lines = (lax.axis_size(axes), shard.reshape(-1, *shard.shape[1:][-1:]))
    parts = padded_to(lines, count).reshape(count, -1, *lines.shape[1:])
    own = sum_in_order(parts, axes, turns)
    whole = gather_in_order(own, axes, turns[::-1]).reshape(-1, *lines.shape[1:])
    return whole[: len(lines)].reshape(shard.shape)


def cut_along(shard, dim, count):
    before, after = (shard.shape[:dim], shard.shape[dim + 1 :])
    return jnp.moveaxis(shard.reshape(*before, count, -1, *after), dim, 0)


def sum_at_owner(shard, axis, dim):
    count = lax.axis_size(axis)
    parts = lax.all_to_all(cut_along(shard, dim, count), axis, 0, 0, tiled=True)
    return jnp.sum(parts, axis=0)


def one_axis_at_a_time(shard, axes):
    for axis in axes:
        shard = lax.psum(shard, axis)
    return shard


def in_order(parts, dim):
    parts = jnp.moveaxis(parts, 0, dim)
    lengths = parts.shape
    return parts.reshape(*lengths[:dim], lengths[dim] * lengths[dim + 1], *lengths[dim + 2 :])


def sent_to_all(shard, axis):
    copies = jnp.broadcast_to(shard, (lax.axis_size(axis), *shard.shape))
    return lax.all_to_all(copies, axis, split_axis=0, concat_axis=0, tiled=True)


def collect(shard, axis, dim):
    return in_order(sent_to_all(shard, axis), dim)


def body(momentum, gradient, right_prev):
    buffer = (momentum.astype(jnp.float32) + gradient.astype(jnp.float32)).astype(jnp.bfloat16)
    partial_value = jnp.dot(
        buffer, right_prev.astype(jnp.bfloat16), preferred_element_type=jnp.float32
    )
    projected = sum_by_parts(partial_value, "narrow")
    gram_part = jnp.dot(projected.T, projected, precision=lax.Precision.HIGHEST)
    gram_matrix = sum_in_two_steps(gram_part, WIDE, (0, 2, 1))
    lower = jnp.linalg.cholesky(gram_matrix)
    left_basis = jax.scipy.linalg.solve_triangular(lower, projected.T, lower=True).T
    right_part = lax.dot_general(
        buffer,
        left_basis.astype(jnp.bfloat16),
        (((0,), (0,)), ((), ())),
        preferred_element_type=jnp.float32,
    )
    share = sum_at_owner(right_part, WIDE, 0)
    column_squares = one_axis_at_a_time(jnp.sum(share * share, axis=0), WIDE_NARROW)
    right_factor = collect(share, WIDE, 0)
    right_next = right_factor / jnp.sqrt(column_squares + 1e-06)
    feedback = jnp.dot(left_basis, right_factor.T, precision=lax.Precision.HIGHEST)
    momentum_next = (buffer.astype(jnp.float32) - 0.05 * feedback).astype(jnp.bfloat16)
    scaling = math.sqrt(FF * D / RANK)
    weight_update = scaling * jnp.dot(left_basis, right_next.T, precision=lax.Precision.HIGHEST)
    return (momentum_next, weight_update, right_next)


def solution(mesh):
    torus = Mesh(
        mesh.devices.reshape(8, 4, 2, mesh.shape["narrow"]),
        ("wide_0", "wide_1", "wide_2", "narrow"),
    )
    in_specs = (P(WIDE, "narrow"), P(WIDE, "narrow"), P("narrow", None))
    out_specs = (P(WIDE, "narrow"), P(WIDE, "narrow"), P("narrow", None))
    return jax.shard_map(body, mesh=torus, in_specs=in_specs, out_specs=out_specs, check_vma=False)
```

profile of v0, /device:TPU:1, one launch (start us, length us, event | category | flops | bytes accessed | tf_op | source)
XLA Modules:
  0.0 504.0 jit_solution(14413329687044880616)
XLA Ops:
  7.2 1.9 fusion.12
  9.2 34.6 %fusion = f32[40,512]{1,0:T(8,128)S(1)} fusion(f32[456,512]{1,0:T(8,128)S(1)} %pad.5), kind=kCustom, calls=%all-reduce-scatter | all-reduce-scatter fusion | flops 245761 | bytes 1019904
  43.8 2.4 collective-permute-start
  46.3 1.3 dynamic-slice.7
  48.2 0.2 concatenate.12
  48.4 21.9 %all-gather = f32[12,38,512]{2,1,0:T(8,128)S(1)} all-gather(f32[1,38,512]{2,1,0:T(8,128)S(1)} %dynamic-slice_bitcast_fusion), channel_id=1, replica_groups=mesh['wide_0'=8,'wide_1'=4,'wide_2'=2,'narrow'=12] {'narrow'}, dimensions={0}, use_global_device_ids=true | all-gather | bytes 1011712 | tf_op jit(solution)/shard_map/all_gather | solution.py:25
  70.4 1.9 fusion.5
  72.4 1.1 copy.10
  73.5 48.4 %reduce-scatter.6.cloned.1.call-done = f32[8,8,512]{2,1,0:T(8,128)} async-done(((f32[64,8,512]{2,1,0:T(8,128)}), f32[8,8,512]{2,1,0:T(8,128)}) %reduce-scatter.6.cloned.1.call-update) | async-done | bytes 131088 | tf_op jit(solution)/shard_map/reduce_scatter | solution.py:34
  122.0 27.4 %reduce-scatter.8.cloned.1.call-done = f32[4,8,512]{2,1,0:T(8,128)} async-done(((f32[8,8,512]{2,1,0:T(8,128)}), f32[4,8,512]{2,1,0:T(8,128)}) %reduce-scatter.8.cloned.1.call-update) | async-done | bytes 65552 | tf_op jit(solution)/shard_map/reduce_scatter | solution.py:34
  149.5 28.6 %reduce-scatter.10.cloned.1.call-done = f32[1,8,512]{2,1,0:T(8,128)} async-done(((f32[4,8,512]{2,1,0:T(8,128)}), f32[1,8,512]{2,1,0:T(8,128)}) %reduce-scatter.10.cloned.1.call-update) | async-done | bytes 16400 | tf_op jit(solution)/shard_map/reduce_scatter | solution.py:34
  178.1 9.2 %all_gather.13 = f32[4,8,512]{2,1,0:T(8,128)S(1)} all-gather(f32[1,8,512]{2,1,0:T(8,128)} %reduce-scatter.10.cloned.1.call-done), channel_id=1, replica_groups=mesh['wide_0'=8,'wide_1'=4,'wide_2'=2,'narrow'=12] {'wide_1'}, dimensions={0}, use_global_device_ids=true | all-gather | bytes 81920 | tf_op jit(solution)/shard_map/all_gather | solution.py:41
  187.3 7.8 %all_gather.14 = f32[8,8,512]{2,1,0:T(8,128)} all-gather(f32[4,8,512]{2,1,0:T(8,128)S(1)} %all_gather.13), channel_id=1, replica_groups=mesh['wide_0'=8,'wide_1'=4,'wide_2'=2,'narrow'=12] {'wide_2'}, dimensions={0}, use_global_device_ids=true | all-gather | bytes 196608 | tf_op jit(solution)/shard_map/all_gather | solution.py:41
  195.3 38.3 %all-gather.3.cloned.1.call-done = f32[64,8,512]{2,1,0:T(8,128)} async-done(((f32[8,8,512]{2,1,0:T(8,128)}), f32[64,8,512]{2,1,0:T(8,128)}) %all-gather.3.cloned.1.call-update) | async-done | bytes 1048592 | tf_op jit(solution)/shard_map/all_gather | solution.py:41
  233.6 1.3 copy.11
  234.9 0.3 copy.12
  235.2 0.2 fusion.4
  235.5 1.0 copy-done.1
  236.5 11.7 %cholesky.104 = f32[128,128]{1,0:T(8,128)S(1)} custom-call(f32[128,128]{1,0:T(8,128)S(1)} %cholesky.266), custom_call_target="Cholesky" | custom-call | tf_op jit(solution)/shard_map/jit(cholesky)/cholesky | solution.py:96
  248.4 9.8 %custom-call.31 = f32[1,128,128]{1,2,0:T(8,128)S(1)} custom-call(f32[1,128,128]{2,1,0:T(8,128)S(1)} %get-tuple-element.30), custom_call_target="InvertDiagBlocksLowerTriangular" | custom-call | tf_op jit(solution)/shard_map/jit(cholesky)/cholesky | solution.py:96
  258.2 0.3 constant_dynamic-update-slice_fusion.3
  258.5 0.3 convolution_subtract_fusion.3
  258.9 11.7 %cholesky.217 = f32[128,128]{1,0:T(8,128)S(1)} custom-call(f32[128,128]{1,0:T(8,128)S(1)} %cholesky.270), custom_call_target="Cholesky" | custom-call | tf_op jit(solution)/shard_map/jit(cholesky)/cholesky | solution.py:96
  270.6 9.9 %custom-call.32 = f32[1,128,128]{1,2,0:T(8,128)S(1)} custom-call(f32[1,128,128]{2,1,0:T(8,128)S(1)} %get-tuple-element.27), custom_call_target="InvertDiagBlocksLowerTriangular" | custom-call | tf_op jit(solution)/shard_map/jit(cholesky)/cholesky | solution.py:96
  280.6 0.3 convolution_dynamic-update-slice_fusion
  280.8 0.4 convolution_subtract_fusion.4
  281.2 11.7 %cholesky.238 = f32[128,128]{1,0:T(8,128)S(1)} custom-call(f32[128,128]{1,0:T(8,128)S(1)} %cholesky.275), custom_call_target="Cholesky" | custom-call | tf_op jit(solution)/shard_map/jit(cholesky)/cholesky | solution.py:96
  293.0 9.8 %custom-call.33 = f32[1,128,128]{1,2,0:T(8,128)S(1)} custom-call(f32[1,128,128]{2,1,0:T(8,128)S(1)} %get-tuple-element.24), custom_call_target="InvertDiagBlocksLowerTriangular" | custom-call | tf_op jit(solution)/shard_map/jit(cholesky)/cholesky | solution.py:96
  302.8 0.2 convolution_dynamic-update-slice_fusion.1
  303.0 0.4 convolution_subtract_fusion.5
  303.4 11.7 %cholesky.255 = f32[128,128]{1,0:T(8,128)S(1)} custom-call(f32[128,128]{1,0:T(8,128)S(1)} %convolution_subtract_fusion.5), custom_call_target="Cholesky" | custom-call | tf_op jit(solution)/shard_map/jit(cholesky)/cholesky | solution.py:96
  315.1 0.7 compare_reduce_fusion.1
  315.9 0.8 compare_reduce_fusion
  316.7 0.7 compare_reduce_fusion.2
  319.9 0.1 select_select_fusion
  320.0 10.9 %while.1 = (s32[]{:T(128)}, f32[512,512]{1,0:T(8,128)S(1)}, s32[4,2]{0,1:T(2,128)S(1)}, f32[4,128,128]{2,1,0:T(8,128)}, s32[]{:T(128)}) while((s32[]{:T(128)}, f32[512,512]{1,0:T(8,128)S(1)}, s32[4,2]{0,1:T(2,128)S(1)}, f32[4,128,128]{2,1,0:T(8,128)}, s32[]{:T(128)}) %tuple.31), condition=%wide.while_cond, body=%wide.while_body.sunk | while | flops 2 | bytes 132205 | solution.py:97
  320.1 0.6 fusion.50
  320.7 2.1 bitcast_dynamic-update-slice_fusion.2
  322.8 0.6 fusion.50
  323.4 2.1 bitcast_dynamic-update-slice_fusion.2
  325.6 0.6 fusion.50
  326.2 2.1 bitcast_dynamic-update-slice_fusion.2
  328.3 0.6 fusion.50
  328.9 2.1 bitcast_dynamic-update-slice_fusion.2
  331.0 40.1 %custom-call.34 = f32[4,128,128]{1,2,0:T(8,128)S(1)} custom-call(f32[4,128,128]{2,1,0:T(8,128)} %get-tuple-element.10), custom_call_target="InvertDiagBlocksLowerTriangular" | custom-call | tf_op jit(solution)/shard_map/jit(_solve_triangular)/triangular_solve | solution.py:97
  371.1 0.3 fusion.19
  371.4 0.4 convolution_subtract_fusion.2
  371.8 0.3 fusion.31
  372.1 0.5 convolution_subtract_fusion.1
  372.7 0.3 fusion.29
  373.0 0.7 convolution_subtract_fusion
  373.8 0.3 fusion.28
  374.1 0.7 copy-done.3
  374.8 0.5 convolution_bitcast_fusion
  375.3 40.8 %all_to_all.10 = f32[64,8,512]{2,1,0:T(8,128)S(1)} all-to-all(f32[64,8,512]{2,1,0:T(8,128)S(1)} %convolution_bitcast_fusion), channel_id=1, replica_groups=mesh['wide_0'=8,'wide_1'=4,'wide_2'=2,'narrow'=12] {'wide_0','wide_1','w..., dimensions={0} | all-to-all | bytes 2097152 | tf_op jit(solution)/shard_map/all_to_all | solution.py:63
  416.2 1.1 broadcast_in_dim.6
  417.3 6.3 %all-to-all-start.1 = ((f32[64,8,512]{2,1,0:T(8,128)}), f32[64,8,512]{2,1,0:T(8,128)S(1)}, u32[]{:S(2)}, u32[]{:S(2)}) async-start(f32[64,8,512]{2,1,0:T(8,128)} %broadcast_in_dim.6), calls=%async_computation.4 | async-start | bytes 2097152 | tf_op jit(solution)/shard_map/all_to_all | solution.py:81
  423.6 32.0 %psum.28 = f32[512]{0:T(512)S(1)} all-reduce(f32[512]{0:T(512)S(1)} %multiply_reduce_fusion), channel_id=1, replica_groups=mesh['wide_0'=8,'wide_1'=4,'wide_2'=2,'narrow'=12] {'wide_0'}, use_global_device_ids=true, to_apply=%region_14.15 | all-reduce | flops 512 | bytes 4096 | tf_op jit(solution)/shard_map/psum | solution.py:69
  455.6 8.2 %psum.29 = f32[512]{0:T(512)S(1)} all-reduce(f32[512]{0:T(512)S(1)} %psum.28), channel_id=1, replica_groups=mesh['wide_0'=8,'wide_1'=4,'wide_2'=2,'narrow'=12] {'wide_1'}, use_global_device_ids=true, to_apply=%region_15.16 | all-reduce | flops 512 | bytes 4096 | tf_op jit(solution)/shard_map/psum | solution.py:69
  463.8 8.2 %psum.30 = f32[512]{0:T(512)S(1)} all-reduce(f32[512]{0:T(512)S(1)} %psum.29), channel_id=1, replica_groups=mesh['wide_0'=8,'wide_1'=4,'wide_2'=2,'narrow'=12] {'wide_2'}, use_global_device_ids=true, to_apply=%region_16.17 | all-reduce | flops 512 | bytes 4096 | tf_op jit(solution)/shard_map/psum | solution.py:69
  472.0 19.9 %psum.31 = f32[512]{0:T(512)S(1)} all-reduce(f32[512]{0:T(512)S(1)} %psum.30), channel_id=1, replica_groups=mesh['wide_0'=8,'wide_1'=4,'wide_2'=2,'narrow'=12] {'narrow'}, use_global_device_ids=true, to_apply=%region_17.18 | all-reduce | flops 512 | bytes 4096 | tf_op jit(solution)/shard_map/psum | solution.py:69
  492.0 0.2 bitcast_divide_fusion
  492.1 2.6 convolution_multiply_fusion
  494.7 2.5 fusion.2
  (43 shorter events, 1.2 us)
Async XLA Ops:
  7.2 114.8 %reduce-scatter.6.cloned.1.call-start = ((), (), s32[]{:S(2)}) async-start(), calls=%async_computation.5 | async-start | bytes 1179648 | tf_op jit(solution)/shard_map/reduce_scatter | solution.py:34
  43.8 4.4 collective-permute-start
  73.5 76.0 %reduce-scatter.8.cloned.1.call-start = ((), (), s32[]{:S(2)}) async-start(), calls=%async_computation.6 | async-start | bytes 196608 | tf_op jit(solution)/shard_map/reduce_scatter | solution.py:34
  122.0 56.2 %reduce-scatter.10.cloned.1.call-start = ((), (), s32[]{:S(2)}) async-start(), calls=%async_computation.7 | async-start | bytes 81920 | tf_op jit(solution)/shard_map/reduce_scatter | solution.py:34
  149.4 84.1 %all-gather.3.cloned.1.call-start = ((), (), s32[]{:S(2)}) async-start(), calls=%async_computation.8 | async-start | bytes 1179648 | tf_op jit(solution)/shard_map/all_gather | solution.py:41
  235.5 1.0 copy-start.1
  236.5 21.7 %copy-start.2 = (f32[512,512]{1,0:T(8,128)S(1)}, f32[512,512]{1,0:T(8,128)}, u32[]{:S(2)}) copy-start(f32[512,512]{1,0:T(8,128)} %copy-done.1) | copy-start | bytes 3145732
  373.0 1.1 copy-start.4
  373.8 1.1 copy-start.3
  417.3 74.7 %all-to-all-start.1 = ((f32[64,8,512]{2,1,0:T(8,128)}), f32[64,8,512]{2,1,0:T(8,128)S(1)}, u32[]{:S(2)}, u32[]{:S(2)}) async-start(f32[64,8,512]{2,1,0:T(8,128)} %broadcast_in_dim.6), calls=%async_computation.4 | async-start | bytes 2097152 | tf_op jit(solution)/shard_map/all_to_all | solution.py:81
  492.1 2.6 copy-start
  492.1 2.6 copy-start.5
Sparse Core Ops, SparseCore 0:
  73.6 48.2 reduce-scatter.5
  125.0 24.4 reduce-scatter.7
  152.5 25.5 reduce-scatter.9
  195.3 38.2 all-gather.2
where the time goes:
time: 511 us; the launch traced here: 504 us
  blocking collectives  183 us (36%)
  waiting for transfers between devices  143 us (28%)
  other arithmetic  120 us (23%)
  local copies, waits for them, and re-layouts  18.2 us (4%)
  between operations  17.6 us (3%)
  matrix products  14.2 us (3%)
  starting transfers between devices  8.84 us (2%)
    reduce_scatter x3, waiting for transfers between devices, sum_in_order(): parts = lax.psum_scatter(parts, axes[k], scatter_dimension=0, tiled=True)  104 us
    another operation x14, other arithmetic, body(): lower = jnp.linalg.cholesky(gram_matrix)  78.8 us
    psum x4, blocking collectives, one_axis_at_a_time(): shard = lax.psum(shard, axis)  68.3 us
    all_to_all x1, blocking collectives, sum_at_owner(): parts = lax.all_to_all(cut_along(shard, dim, count), axis, 0, 0, tiled=True)  40.8 us
    another operation x3, other arithmetic, body(): jax.scipy.linalg.solve_triangular(lower, projected.T, lower=True)  40.3 us
    all_gather x1, waiting for transfers between devices, gather_in_order(): parts = lax.all_gather(parts, axes[k], axis=0, tiled=True)  38.3 us
    unnamed x1, blocking collectives  34.6 us
    all_gather x1, blocking collectives, sum_by_parts(): whole = lax.all_gather(own, axis, axis=0, tiled=True)  21.9 us
  transfers between devices with their start and end apart: 6, of which 4 were waited for; matrix products, arithmetic and copies ran while one was open for 0% of the time, Pallas kernels for 0%

commit v1 on v0

v1 whole, which is shorter than its diff:
```python
import functools
import math

import jax
import jax.numpy as jnp
from jax import lax
from jax.experimental import pallas as pl
from jax.experimental.pallas import tpu as pltpu
from jax.sharding import Mesh
from jax.sharding import PartitionSpec as P

FF = 28672
D = 6144
RANK = 512
BLK = 128
F32 = jnp.float32
BF16 = jnp.bfloat16
NN = ((1,), (0,))
NT = ((1,), (1,))
MESH = pl.DeviceIdType.MESH


def split(x):
    high = x.astype(BF16)
    return high, (x - high.astype(F32)).astype(BF16)


def mm(a, b, dims):
    return lax.dot_general(a, b, (dims, ((), ())), preferred_element_type=F32)


def mm3(a, b, dims):
    (ah, al), (bh, bl) = a, b
    return mm(ah, bh, dims) + (mm(ah, bl, dims) + mm(al, bh, dims))


def lane(x, k):
    return jnp.broadcast_to(x[:, k : k + 1], (8, BLK))


def sublane(x, k):
    return jnp.broadcast_to(x[k : k + 1, :], (8, BLK))


def tree_sum(terms):
    while len(terms) > 1:
        odd = terms[len(terms) & ~1 :]
        terms = [terms[i] + terms[i + 1] for i in range(0, len(terms) & ~1, 2)] + odd
    return terms[0]


def inverse_factor(rows):
    row_id = lax.broadcasted_iota(jnp.int32, (8, BLK), 0)
    lane_id = lax.broadcasted_iota(jnp.int32, (8, BLK), 1)
    count = len(rows)
    a = list(rows)
    e = [(lane_id == row_id + 8 * r).astype(F32) for r in range(count)]
    for r in range(count):
        cols = [lane(a[r], 8 * r + k) for k in range(8)]
        full_a, full_e, forward = a[r], e[r], e[r]
        pivots = jnp.ones((8, BLK), F32)
        for j in range(0, 8, 2):
            p, q, w = sublane(cols[j], j), sublane(cols[j + 1], j), sublane(cols[j + 1], j + 1)
            inv = 1.0 / (p * w - q * q)
            first, second = row_id == j, row_id == j + 1
            pair = first | second
            c1, c2 = cols[j], cols[j + 1]
            m1 = inv * jnp.where(first, -w, jnp.where(second, q, c1 * w - c2 * q))
            m2 = inv * jnp.where(first, q, jnp.where(second, -p, c2 * p - c1 * q))

            def solve(v):
                return jnp.where(pair, 0.0, v) - (m1 * sublane(v, j) + m2 * sublane(v, j + 1))

            ratio = q / p
            f1 = sublane(forward, j)
            f2 = sublane(forward, j + 1)
            below = m1 * f1 + m2 * f2
            forward = forward - jnp.where(
                row_id > j + 1, below, jnp.where(second, ratio * f1, 0.0)
            )
            pivots = jnp.where(first, p, jnp.where(second, w - q * ratio, pivots))
            for k in range(j + 2, 8):
                cols[k] = solve(cols[k])
            full_a, full_e = solve(full_a), solve(full_e)
        e[r] = forward * lax.rsqrt(pivots)
        if r == count - 1:
            break
        row_a = [sublane(full_a, k) for k in range(8)]
        row_e = [sublane(full_e, k) for k in range(8)]
        for s in range(r + 1, count):
            col = [lane(a[s], 8 * r + k) for k in range(8)]
            for k in range(8):
                a[s] = a[s] - col[k] * row_a[k]
                e[s] = e[s] - col[k] * row_e[k]
    return e


class Copies:
    def __init__(self, send, recv):
        self.send, self.recv, self.made = send, recv, {}

    def copy(self, key):
        at, make = self.made[key]
        src, dst, where = make()
        return pltpu.make_async_remote_copy(
            src_ref=src,
            dst_ref=dst,
            send_sem=self.send.at[at],
            recv_sem=self.recv.at[at],
            device_id=where,
            device_id_type=MESH,
        )

    def start(self, key, make):
        self.made[key] = (len(self.made), make)
        self.copy(key).start()

    def arrived(self, key):
        self.copy(key).wait_recv()

    def sent(self):
        for key in self.made:
            self.copy(key).wait_send()


class PlaneSum:
    def __init__(self, sizes, me, part, whole, from_c, from_x, from_y, send, recv):
        self.ny, self.nx, self.nc, _ = sizes
        self.y, self.x, self.c = me
        self.part, self.whole = part, whole
        self.from_c, self.from_x, self.from_y = from_c, from_x, from_y
        rows = part.shape[0]
        self.hc, self.hx, self.hy = rows // 2, rows // 2 // self.nx, rows // 2 // self.nx // self.ny
        self.at_c = self.c * self.hc
        self.at_x = self.at_c + self.x * self.hx
        self.at_y = self.at_x + self.y * self.hy
        self.copies = Copies(send, recv)

    def rows(self, ref, at, count):
        return ref.at[pl.ds(pl.multiple_of(at, 8), count)]

    def send_c(self):
        def make():
            other = (1 - self.c) * self.hc
            return self.rows(self.part, other, self.hc), self.from_c, {"c": 1 - self.c}

        self.copies.start("c", make)

    def deal(self, axis, n, me, at, count, dst):
        for d in range(1, n):

            def make(d=d):
                peer = lax.rem(me + d, n)
                return self.rows(self.part, at + peer * count, count), dst.at[d - 1], {axis: peer}

            self.copies.start((axis, d), make)

    def send_x(self):
        self.copies.arrived("c")
        own = self.rows(self.part, self.at_c, self.hc)
        own[...] += self.from_c[...]
        self.deal("x", self.nx, self.x, self.at_c, self.hx, self.from_x)

    def send_y(self):
        own = self.rows(self.part, self.at_x, self.hx)
        for d in range(1, self.nx):
            self.copies.arrived(("x", d))
        own[...] = tree_sum([own[...]] + [self.from_x[d] for d in range(self.nx - 1)])
        self.deal("y", self.ny, self.y, self.at_x, self.hy, self.from_y)

    def spread(self, axis, n, me, at, count):
        for d in range(1, n):

            def make(d=d):
                block = self.rows(self.whole, at, count)
                return block, block, {axis: lax.rem(me + d, n)}

            self.copies.start((axis + "w", d), make)

    def plane_total(self):
        own = self.rows(self.part, self.at_y, self.hy)
        for d in range(1, self.ny):
            self.copies.arrived(("y", d))
        return tree_sum([own[...]] + [self.from_y[d] for d in range(self.ny - 1)])

    def spread_y(self, total):
        self.whole[pl.ds(pl.multiple_of(self.at_y, 8), self.hy)] = total
        self.spread("y", self.ny, self.y, self.at_y, self.hy)

    def spread_x(self):
        for d in range(1, self.ny):
            self.copies.arrived(("yw", d))
        self.spread("x", self.nx, self.x, self.at_x, self.hx)

    def spread_c(self):
        for d in range(1, self.nx):
            self.copies.arrived(("xw", d))
        self.spread("c", 2, self.c, self.at_c, self.hc)

    def finish(self):
        self.copies.arrived(("cw", 1))
        self.copies.sent()

    @staticmethod
    def count(sizes):
        ny, nx, _, _ = sizes
        return 2 * (1 + (nx - 1) + (ny - 1))


def kernel(
    sizes,
    m_in, g_in, r_in,
    qb_out, fac_out, inv_out,
    m_ref, g_ref, r_ref, buft, part, steps, flat, own, ph, pl_,
    gpart, gwhole, g_c, g_x, g_y, g_own, g_z,
    hpart, hwhole, h_c, h_x, h_y,
    work, inv_blk, qb, fac, squares, others,
    io, zs_send, zs_recv, zg_send, zg_recv, g_send, g_recv, z_send, z_recv,
    h_send, h_recv, q_send, q_recv,
):
    ny, nx, nc, nz = sizes
    y, x, c, z = (lax.axis_index(a) for a in ("y", "x", "c", "z"))
    rows = m_ref.shape[0]
    rank = RANK
    blocks = rank // BLK
    half = rank // 2

    barrier = pltpu.get_barrier_semaphore()
    greeted = 0
    for axis, n, me in (("c", nc, c), ("x", nx, x), ("y", ny, y), ("z", nz, z)):
        for d in range(1, n):
            pl.semaphore_signal(
                barrier, inc=1, device_id={axis: lax.rem(me + d, n)}, device_id_type=MESH
            )
            greeted += 1
    loads = [
        pltpu.make_async_copy(src, dst, io.at[k])
        for k, (src, dst) in enumerate(((m_in, m_ref), (g_in, g_ref), (r_in, r_ref)))
    ]
    for load in loads:
        load.start()
    for load in loads:
        load.wait()

    b = (m_ref[...].astype(F32) + g_ref[...].astype(F32)).astype(BF16)
    chunk = part.shape[0] // nz
    part[0:rows] = mm(b, r_ref[...].astype(BF16), NN)
    if part.shape[0] > rows:
        part[rows:] = jnp.zeros((part.shape[0] - rows, rank), F32)
    pl.semaphore_wait(barrier, greeted)

    tiles = chunk // 8
    cuts = [(int(2 * k >= tiles), 8 * k) for k in range(tiles)]
    longer, shorter = nz // 2, nz - 1 - nz // 2
    hops = lambda way, group: longer if way == group else shorter
    ahead = lambda way, d: lax.rem(z + d, nz) if way == 0 else lax.rem(z + nz - d, nz)
    rows_at = lambda owner, at: pl.ds(pl.multiple_of(owner * chunk + at, 8), 8)
    sums = Copies(zs_send, zs_recv)
    for t in range(1, longer + 1):
        for k, (group, at) in enumerate(cuts):
            for way in range(2):
                length = hops(way, group)
                if t > length:
                    continue
                src = part.at[rows_at(ahead(way, length - t + 1), at)]
                if t > 1:
                    sums.arrived((way, t - 1, k))
                    held = steps.at[way, t - 2, pl.ds(at, 8)]
                    held[...] += src[...]
                    src = held
                dst = steps.at[way, t - 1, pl.ds(at, 8)]
                where = {"z": ahead(way, 1)}
                sums.start((way, t, k), lambda a=src, b=dst, c=where: (a, b, c))
        if t == 1:
            buft[...] = jnp.transpose(b.astype(F32)).astype(BF16)
            work[...] = jnp.zeros((rank, rank), F32)
            own[...] = jnp.zeros((BLK, rank), F32)

    gather = Copies(zg_send, zg_recv)
    for k, (group, at) in enumerate(cuts):
        terms = [part[rows_at(z, at)]]
        for way in range(2):
            length = hops(way, group)
            if length:
                sums.arrived((way, length, k))
                terms.append(steps[way, length - 1, pl.ds(at, 8)])
        total = tree_sum(terms)
        flat[rows_at(z, at)] = total
        own[at : at + 8] = total
        piece = flat.at[rows_at(z, at)]
        for way in range(2):
            if hops(way, group):
                where = {"z": ahead(way, 1)}
                gather.start((way, 1, k), lambda a=piece, c=where: (a, a, c))

    def relay(t):
        for k, (group, at) in enumerate(cuts):
            for way in range(2):
                length = hops(way, group)
                if t > length + 1:
                    continue
                gather.arrived((way, t - 1, k))
                if t <= length:
                    piece = flat.at[rows_at(ahead(1 - way, t - 1), at)]
                    where = {"z": ahead(way, 1)}
                    gather.start((way, t, k), lambda a=piece, c=where: (a, a, c))

    high, low = split(own[...])
    high_t, low_t = split(jnp.transpose(own[...]))
    for top in range(2):
        first = half * top
        gram = mm3(
            (high_t[first : first + half], low_t[first : first + half]),
            (high[:, first:], low[:, first:]),
            NN,
        )
        for k in range((rank - first) // BLK):
            at = top * blocks * half + half * k
            gpart[at : at + half] = gram[:, BLK * k : BLK * (k + 1)]
    gsum = PlaneSum(sizes, (y, x, c), gpart, gwhole, g_c, g_x, g_y, g_send, g_recv)
    hsum = PlaneSum(sizes, (y, x, c), hpart, hwhole, h_c, h_x, h_y, h_send, h_recv)
    gsum.send_c()
    relay(2)
    gsum.send_x()
    for t in range(3, longer + 2):
        if t == 5:
            gsum.send_y()
        if t < longer + 1:
            relay(t)
    if longer + 1 < 6:
        gsum.send_y()
    g_own[...] = gsum.plane_total()
    across = Copies(z_send, z_recv)
    for d in range(1, nz):
        where = {"z": lax.rem(z + d, nz)}
        across.start(d, lambda d=d, c=where: (g_own, g_z.at[d - 1], c))
    if longer > 1:
        relay(longer + 1)

    for k in range(blocks):
        cols = slice(BLK * k, BLK * (k + 1))
        ph[:, cols], pl_[:, cols] = split(flat[0:rows, cols])
    product = mm(buft[...], ph[...], NN) + mm(buft[...], pl_[...], NN)
    for k in range(blocks):
        hpart[rank * k : rank * (k + 1)] = product[:, BLK * k : BLK * (k + 1)]
    hsum.send_c()
    hsum.send_x()
    for d in range(1, nz):
        across.arrived(d)
    gsum.spread_y(tree_sum([g_own[...]] + [g_z[d] for d in range(nz - 1)]))
    hsum.send_y()
    gsum.spread_x()
    hsum.spread_y(hsum.plane_total())
    gsum.spread_c()
    gsum.finish()
    for k in range(blocks):
        work[0:half, BLK * k : BLK * (k + 1)] = gwhole[half * k : half * (k + 1)]
    for k in range(blocks // 2):
        at = blocks * half + half * k
        work[half:rank, half + BLK * k : half + BLK * (k + 1)] = gwhole[at : at + half]

    eye = lax.broadcasted_iota(jnp.int32, (BLK, BLK), 0) == lax.broadcasted_iota(
        jnp.int32, (BLK, BLK), 1
    )

    @pl.loop(0, blocks)
    def _(at):
        r0 = pl.multiple_of(at * BLK, BLK)
        band = pl.ds(r0, BLK)
        diagonal = [work[pl.ds(pl.multiple_of(r0 + 8 * r, 8), 8), band] for r in range(BLK // 8)]
        for r, tile in enumerate(inverse_factor(diagonal)):
            inv_blk[8 * r : 8 * r + 8, :] = tile
        pl.when(at == 0)(hsum.spread_x)
        pl.when(at == 2)(hsum.spread_c)
        work[band, band] = eye.astype(F32)
        solved = mm3(split(inv_blk[...]), split(work[band, :]), NN)
        work[band, :] = solved
        right = split(solved)

        @pl.loop(at + 1, blocks)
        def _(below):
            under = pl.ds(pl.multiple_of(below * BLK, BLK), BLK)
            left = split(jnp.transpose(work[band, under]))
            work[under, band] = jnp.zeros((BLK, BLK), F32)
            work[under, :] -= mm3(left, right, NN)

    block_of = lambda dim: lax.broadcasted_iota(jnp.int32, (rank, rank), dim) // BLK
    inverse = split(jnp.where(block_of(0) >= block_of(1), work[...], 0.0))
    qb[...] = mm3((ph[...], pl_[...]), inverse, NT).astype(BF16)
    stores = [pltpu.make_async_copy(qb, qb_out, io.at[0])]
    stores[0].start()
    hsum.finish()
    whole = jnp.concatenate([hwhole[rank * k : rank * (k + 1)] for k in range(blocks)], axis=1)
    factor = mm3(split(whole), inverse, NT)
    squares[...] = jnp.sum(factor * factor, axis=0, keepdims=True)
    totals = Copies(q_send, q_recv)
    for d in range(1, nz):
        where = {"z": lax.rem(z + d, nz)}
        totals.start(d, lambda d=d, c=where: (squares, others.at[d - 1], c))
    fac[...] = factor
    stores.append(pltpu.make_async_copy(fac, fac_out, io.at[1]))
    stores[1].start()
    for d in range(1, nz):
        totals.arrived(d)
    total = tree_sum([squares[...]] + [others[d] for d in range(nz - 1)])
    inv_out[...] = 1.0 / jnp.sqrt(total + 1e-06)
    for store in stores:
        store.wait()
    for copies in (sums, gather, across, totals):
        copies.sent()


def outputs(m_ref, g_ref, q_ref, f_ref, inv_ref, mn_ref, wu_ref, rn_ref):
    step = pl.program_id(0)
    count = rn_ref.shape[0]
    b = (m_ref[...].astype(F32) + g_ref[...].astype(F32)).astype(BF16)
    feedback = mm(q_ref[...], f_ref[...].astype(BF16), NT)
    mn_ref[...] = (b.astype(F32) - 0.05 * feedback).astype(BF16)
    following = f_ref[...] * inv_ref[...]
    scaling = math.sqrt(FF * D / RANK)
    wu_ref[...] = scaling * mm(q_ref[...], following.astype(BF16), NT)
    rn_ref[...] = f_ref[pl.ds(pl.multiple_of(step * count, 8), count), :] * inv_ref[...]


def body(sizes, momentum, gradient, right_prev):
    ny, nx, nc, nz = sizes
    rows, cols = momentum.shape
    rank = right_prev.shape[1]
    blocks = rank // BLK
    chunk = -(-rows // (8 * nz)) * 8
    longer = nz // 2
    hops = (nz - 1) * (chunk // 8)
    g_rows, h_rows = 3 * rank, blocks * cols
    vmem = pltpu.VMEM

    def plane(count):
        half = count // 2
        return [
            vmem((count, BLK), F32),
            vmem((count, BLK), F32),
            vmem((half, BLK), F32),
            vmem((max(nx - 1, 1), half // nx, BLK), F32),
            vmem((max(ny - 1, 1), half // nx // ny, BLK), F32),
        ]

    def sems(count):
        return [pltpu.SemaphoreType.DMA((count,))] * 2

    piece = g_rows // 2 // nx // ny
    basis, factor, norms = pl.pallas_call(
        functools.partial(kernel, sizes),
        out_shape=(
            jax.ShapeDtypeStruct((rows, rank), BF16),
            jax.ShapeDtypeStruct((cols, rank), F32),
            jax.ShapeDtypeStruct((1, rank), F32),
        ),
        in_specs=[pl.BlockSpec(memory_space=pl.ANY)] * 3,
        out_specs=[pl.BlockSpec(memory_space=pl.ANY)] * 2 + [pl.BlockSpec(memory_space=vmem)],
        scratch_shapes=[
            vmem((rows, cols), BF16),
            vmem((rows, cols), BF16),
            vmem((cols, rank), F32),
            vmem((cols, rows), BF16),
            vmem((chunk * nz, rank), F32),
            vmem((2, longer, chunk, rank), F32),
            vmem((chunk * nz, rank), F32),
            vmem((BLK, rank), F32),
            vmem((rows, rank), BF16),
            vmem((rows, rank), BF16),
            *plane(g_rows),
            vmem((piece, BLK), F32),
            vmem((nz - 1, piece, BLK), F32),
            *plane(h_rows),
            vmem((rank, rank), F32),
            vmem((BLK, BLK), F32),
            vmem((rows, rank), BF16),
            vmem((cols, rank), F32),
            vmem((1, rank), F32),
            vmem((nz - 1, 1, rank), F32),
            pltpu.SemaphoreType.DMA((3,)),
            *sems(hops),
            *sems(hops),
            *sems(PlaneSum.count(sizes)),
            *sems(nz - 1),
            *sems(PlaneSum.count(sizes)),
            *sems(nz - 1),
        ],
        compiler_params=pltpu.CompilerParams(collective_id=0, has_side_effects=True),
    )(momentum, gradient, right_prev)

    parts = 4
    row_block = lambda width: pl.BlockSpec((rows // parts, width), lambda i: (i, 0))
    return pl.pallas_call(
        outputs,
        grid=(parts,),
        out_shape=(
            jax.ShapeDtypeStruct((rows, cols), BF16),
            jax.ShapeDtypeStruct((rows, cols), F32),
            jax.ShapeDtypeStruct((cols, rank), F32),
        ),
        in_specs=[
            row_block(cols),
            row_block(cols),
            row_block(rank),
            pl.BlockSpec((cols, rank), lambda i: (0, 0)),
            pl.BlockSpec((1, rank), lambda i: (0, 0)),
        ],
        out_specs=[
            row_block(cols),
            row_block(cols),
            pl.BlockSpec((cols // parts, rank), lambda i: (i, 0)),
        ],
    )(momentum, gradient, basis, factor, norms)


def solution(mesh):
    sizes = (8, 4, 2, mesh.shape["narrow"])
    torus = Mesh(mesh.devices.reshape(sizes), ("y", "x", "c", "z"))
    wide = ("y", "x", "c")
    in_specs = (P(wide, "z"), P(wide, "z"), P("z", None))
    out_specs = (P(wide, "z"), P(wide, "z"), P("z", None))
    return jax.shard_map(
        functools.partial(body, sizes),
        mesh=torus,
        in_specs=in_specs,
        out_specs=out_specs,
        check_vma=False,
    )
```

time: 511 us -> 112 us (0.22); the launches traced: 504 us -> 112 us
  blocking collectives: 183 us -> 0 us
  waiting for transfers between devices: 143 us -> 0 us
  other arithmetic: 120 us -> 0 us
  Pallas kernels: 0 us -> 111 us
  local copies, waits for them, and re-layouts: 18.2 us -> 0 us
  between operations: 17.6 us -> 0.64 us
  matrix products: 14.2 us -> 0 us
  starting transfers between devices: 8.84 us -> 0 us
    another operation x17 -> x0, other arithmetic: 119 us -> none  [the longest x14 78.8 us: body(): lower = jnp.linalg.cholesky(gram_matrix)]
    pallas_call x0 -> x2, Pallas kernels: none -> 111 us  [the longest x1 106 us: body(): pl.pallas_call(functools.partial(kernel, sizes), out_shape=(jax.ShapeDtyp...]
    reduce_scatter x3 -> x0, waiting for transfers between devices: 104 us -> none  [sum_in_order(): parts = lax.psum_scatter(parts, axes[k], scatter_dimension=0, tiled=True)]
    psum x4 -> x0, blocking collectives: 68.3 us -> none  [one_axis_at_a_time(): shard = lax.psum(shard, axis)]
    all_to_all x1 -> x0, blocking collectives: 40.8 us -> none  [sum_at_owner(): parts = lax.all_to_all(cut_along(shard, dim, count), axis, 0, 0, tiled=True)]
    all_gather x3 -> x0, blocking collectives: 38.9 us -> none  [the longest x1 21.9 us: sum_by_parts(): whole = lax.all_gather(own, axis, axis=0, tiled=True)]
    all_gather x1 -> x0, waiting for transfers between devices: 38.3 us -> none  [gather_in_order(): parts = lax.all_gather(parts, axes[k], axis=0, tiled=True)]
    unnamed x1 -> x0, blocking collectives: 34.6 us -> none
  transfers between devices with their start and end apart: 6 -> 0, of which waited for: 4 -> 0; matrix products, arithmetic and copies ran while one was open for 0% -> 0% of each run, Pallas kernels for 0% -> 0%
where the time goes in v1:
time: 112 us
  Pallas kernels  111 us (99%)
    pallas_call x1, Pallas kernels, body(): pl.pallas_call(functools.partial(kernel, sizes), out_shape=(jax.ShapeDtyp...  106 us
    pallas_call x1, Pallas kernels, body(): pl.pallas_call(outputs, grid=(parts,), out_shape=(jax.ShapeDtypeStruct((r...  5.07 us

profile of v1, /device:TPU:1, one launch (start us, length us, event | category | flops | bytes accessed | tf_op | source)
XLA Modules:
  0.0 111.5 jit_solution(4376466235174718517)
XLA Ops:
  0.6 105.8 %shard_map.58 = (bf16[448,512]{1,0:T(8,128)(2,1)}, f32[512,512]{1,0:T(8,128)}, f32[1,512]{1,0:T(1,128)}) custom-call(bf16[448,512]{1,0:T(8,128)(2,1)} %m_ref.1, bf16[448,512]{1,0:T(8,128)(2,1)} %g_ref.1, f32[512,512]{1,0:T(8,128)} %r_in.1), custom_call_target="tpu_custom_call" | custom-call | tf_op jit(solution)/shard_map/pallas_call | solution.py:450
  106.5 5.1 %shard_map.59 = (bf16[448,512]{1,0:T(8,128)(2,1)}, f32[448,512]{1,0:T(8,128)}, f32[512,512]{1,0:T(8,128)}) custom-call(bf16[448,512]{1,0:T(8,128)(2,1)} %m_ref.1, bf16[448,512]{1,0:T(8,128)(2,1)} %g_ref.1, bf16[448,512]{1,0:T(8,128)(2,1)} %get-tuple-element.6.q_ref, f32[512,512]{1,0:T(8,128)} %get-tuple-element.7.f_ref, f32[1,512]{1,0:T(1,128)} %get-tuple-element.8.inv_ref), custom_call_target="tpu_custom_call" | custom-call | tf_op jit(solution)/shard_map/pallas_call | solution.py:493

commit v2 on v1

--- a/solution.py
+++ b/solution.py
@@ -18,6 +18,7 @@
 NN = ((1,), (0,))
 NT = ((1,), (1,))
 MESH = pl.DeviceIdType.MESH
+PARENT = (None, 0, 1, 2, 2, 4, 4)
 
 
 def split(x):
@@ -210,11 +211,11 @@
 def kernel(
     sizes,
     m_in, g_in, r_in,
-    qb_out, fac_out, inv_out,
+    fac_out, fact_out, qb_out, mn_out, inv_out,
     m_ref, g_ref, r_ref, buft, part, steps, flat, own, ph, pl_,
     gpart, gwhole, g_c, g_x, g_y, g_own, g_z,
     hpart, hwhole, h_c, h_x, h_y,
-    work, inv_blk, qb, fac, squares, others,
+    work, inv_blk, qb, mn, fac, fact, squares, others,
     io, zs_send, zs_recv, zg_send, zg_recv, g_send, g_recv, z_send, z_recv,
     h_send, h_recv, q_send, q_recv,
 ):
@@ -256,54 +257,54 @@
     ahead = lambda way, d: lax.rem(z + d, nz) if way == 0 else lax.rem(z + nz - d, nz)
     rows_at = lambda owner, at: pl.ds(pl.multiple_of(owner * chunk + at, 8), 8)
     sums = Copies(zs_send, zs_recv)
-    for t in range(1, longer + 1):
+    kids = lambda at, length: [u for u in range(at + 1, length + 1) if PARENT[u] == at]
+    for s in (6, 5, 3, 4, 2, 1):
         for k, (group, at) in enumerate(cuts):
             for way in range(2):
                 length = hops(way, group)
-                if t > length:
+                if s > length:
                     continue
-                src = part.at[rows_at(ahead(way, length - t + 1), at)]
-                if t > 1:
-                    sums.arrived((way, t - 1, k))
-                    held = steps.at[way, t - 2, pl.ds(at, 8)]
-                    held[...] += src[...]
-                    src = held
-                dst = steps.at[way, t - 1, pl.ds(at, 8)]
-                where = {"z": ahead(way, 1)}
-                sums.start((way, t, k), lambda a=src, b=dst, c=where: (a, b, c))
-        if t == 1:
+                src = part.at[rows_at(ahead(way, s), at)]
+                below = kids(s, length)
+                if below:
+                    for u in below:
+                        sums.arrived((way, u, k))
+                    held = [steps.at[way, u - 1, pl.ds(at, 8)] for u in below]
+                    held[0][...] = tree_sum([src[...]] + [h[...] for h in held])
+                    src = held[0]
+                dst = steps.at[way, s - 1, pl.ds(at, 8)]
+                where = {"z": ahead(way, s - PARENT[s])}
+                sums.start((way, s, k), lambda a=src, b=dst, c=where: (a, b, c))
+        if s == 3:
             buft[...] = jnp.transpose(b.astype(F32)).astype(BF16)
             work[...] = jnp.zeros((rank, rank), F32)
             own[...] = jnp.zeros((BLK, rank), F32)
 
     gather = Copies(zg_send, zg_recv)
+
+    def relay(s):
+        for k, (group, at) in enumerate(cuts):
+            for way in range(2):
+                length = hops(way, group)
+                if s > length:
+                    continue
+                if s:
+                    gather.arrived((way, s, k))
+                piece = flat.at[rows_at(ahead(1 - way, s), at)]
+                for u in kids(s, length):
+                    where = {"z": ahead(way, u - s)}
+                    gather.start((way, u, k), lambda a=piece, c=where: (a, a, c))
+
     for k, (group, at) in enumerate(cuts):
         terms = [part[rows_at(z, at)]]
         for way in range(2):
-            length = hops(way, group)
-            if length:
-                sums.arrived((way, length, k))
-                terms.append(steps[way, length - 1, pl.ds(at, 8)])
+            if hops(way, group):
+                sums.arrived((way, 1, k))
+                terms.append(steps[way, 0, pl.ds(at, 8)])
         total = tree_sum(terms)
         flat[rows_at(z, at)] = total
         own[at : at + 8] = total
-        piece = flat.at[rows_at(z, at)]
-        for way in range(2):
-            if hops(way, group):
-                where = {"z": ahead(way, 1)}
-                gather.start((way, 1, k), lambda a=piece, c=where: (a, a, c))
-
-    def relay(t):
-        for k, (group, at) in enumerate(cuts):
-            for way in range(2):
-                length = hops(way, group)
-                if t > length + 1:
-                    continue
-                gather.arrived((way, t - 1, k))
-                if t <= length:
-                    piece = flat.at[rows_at(ahead(1 - way, t - 1), at)]
-                    where = {"z": ahead(way, 1)}
-                    gather.start((way, t, k), lambda a=piece, c=where: (a, a, c))
+    relay(0)
 
     high, low = split(own[...])
     high_t, low_t = split(jnp.transpose(own[...]))
@@ -320,22 +321,17 @@
     gsum = PlaneSum(sizes, (y, x, c), gpart, gwhole, g_c, g_x, g_y, g_send, g_recv)
     hsum = PlaneSum(sizes, (y, x, c), hpart, hwhole, h_c, h_x, h_y, h_send, h_recv)
     gsum.send_c()
+    gsum.send_x()
+    relay(1)
+    gsum.send_y()
     relay(2)
-    gsum.send_x()
-    for t in range(3, longer + 2):
-        if t == 5:
-            gsum.send_y()
-        if t < longer + 1:
-            relay(t)
-    if longer + 1 < 6:
-        gsum.send_y()
     g_own[...] = gsum.plane_total()
     across = Copies(z_send, z_recv)
     for d in range(1, nz):
         where = {"z": lax.rem(z + d, nz)}
         across.start(d, lambda d=d, c=where: (g_own, g_z.at[d - 1], c))
-    if longer > 1:
-        relay(longer + 1)
+    for s in (4, 3, 5, 6):
+        relay(s)
 
     for k in range(blocks):
         cols = slice(BLK * k, BLK * (k + 1))
@@ -386,9 +382,6 @@
 
     block_of = lambda dim: lax.broadcasted_iota(jnp.int32, (rank, rank), dim) // BLK
     inverse = split(jnp.where(block_of(0) >= block_of(1), work[...], 0.0))
-    qb[...] = mm3((ph[...], pl_[...]), inverse, NT).astype(BF16)
-    stores = [pltpu.make_async_copy(qb, qb_out, io.at[0])]
-    stores[0].start()
     hsum.finish()
     whole = jnp.concatenate([hwhole[rank * k : rank * (k + 1)] for k in range(blocks)], axis=1)
     factor = mm3(split(whole), inverse, NT)
@@ -398,8 +391,20 @@
         where = {"z": lax.rem(z + d, nz)}
         totals.start(d, lambda d=d, c=where: (squares, others.at[d - 1], c))
     fac[...] = factor
-    stores.append(pltpu.make_async_copy(fac, fac_out, io.at[1]))
-    stores[1].start()
+    fact[...] = jnp.transpose(factor).astype(BF16)
+    qb[...] = mm3((ph[...], pl_[...]), inverse, NT).astype(BF16)
+    stores = [
+        pltpu.make_async_copy(src, dst, io.at[k])
+        for k, (src, dst) in enumerate(
+            ((fac, fac_out), (fact, fact_out), (qb, qb_out), (mn, mn_out))
+        )
+    ]
+    for store in stores[:3]:
+        store.start()
+    b = (m_ref[...].astype(F32) + g_ref[...].astype(F32)).astype(BF16)
+    feedback = mm(qb[...], fact[...], NN)
+    mn[...] = (b.astype(F32) - 0.05 * feedback).astype(BF16)
+    stores[3].start()
     for d in range(1, nz):
         totals.arrived(d)
     total = tree_sum([squares[...]] + [others[d] for d in range(nz - 1)])
@@ -410,16 +415,12 @@
         copies.sent()
 
 
-def outputs(m_ref, g_ref, q_ref, f_ref, inv_ref, mn_ref, wu_ref, rn_ref):
-    step = pl.program_id(0)
-    count = rn_ref.shape[0]
-    b = (m_ref[...].astype(F32) + g_ref[...].astype(F32)).astype(BF16)
-    feedback = mm(q_ref[...], f_ref[...].astype(BF16), NT)
-    mn_ref[...] = (b.astype(F32) - 0.05 * feedback).astype(BF16)
-    following = f_ref[...] * inv_ref[...]
-    scaling = math.sqrt(FF * D / RANK)
-    wu_ref[...] = scaling * mm(q_ref[...], following.astype(BF16), NT)
-    rn_ref[...] = f_ref[pl.ds(pl.multiple_of(step * count, 8), count), :] * inv_ref[...]
+def outputs(mn_in, q_ref, ft_ref, f_ref, inv_ref, mn_ref, wu_ref, rn_ref):
+    inv = inv_ref[...]
+    mn_ref[...] = mn_in[...]
+    rn_ref[...] = f_ref[...] * inv
+    scaled = q_ref[...].astype(F32) * (inv * math.sqrt(FF * D / RANK))
+    wu_ref[...] = mm(scaled.astype(BF16), ft_ref[...], NN)
 
 
 def body(sizes, momentum, gradient, right_prev):
@@ -447,15 +448,17 @@
         return [pltpu.SemaphoreType.DMA((count,))] * 2
 
     piece = g_rows // 2 // nx // ny
-    basis, factor, norms = pl.pallas_call(
+    factor, factor_t, basis, following, norms = pl.pallas_call(
         functools.partial(kernel, sizes),
         out_shape=(
+            jax.ShapeDtypeStruct((cols, rank), F32),
+            jax.ShapeDtypeStruct((rank, cols), BF16),
             jax.ShapeDtypeStruct((rows, rank), BF16),
-            jax.ShapeDtypeStruct((cols, rank), F32),
+            jax.ShapeDtypeStruct((rows, cols), BF16),
             jax.ShapeDtypeStruct((1, rank), F32),
         ),
         in_specs=[pl.BlockSpec(memory_space=pl.ANY)] * 3,
-        out_specs=[pl.BlockSpec(memory_space=pl.ANY)] * 2 + [pl.BlockSpec(memory_space=vmem)],
+        out_specs=[pl.BlockSpec(memory_space=pl.ANY)] * 4 + [pl.BlockSpec(memory_space=vmem)],
         scratch_shapes=[
             vmem((rows, cols), BF16),
             vmem((rows, cols), BF16),
@@ -474,10 +477,12 @@
             vmem((rank, rank), F32),
             vmem((BLK, BLK), F32),
             vmem((rows, rank), BF16),
+            vmem((rows, cols), BF16),
             vmem((cols, rank), F32),
+            vmem((rank, cols), BF16),
             vmem((1, rank), F32),
             vmem((nz - 1, 1, rank), F32),
-            pltpu.SemaphoreType.DMA((3,)),
+            pltpu.SemaphoreType.DMA((4,)),
             *sems(hops),
             *sems(hops),
             *sems(PlaneSum.count(sizes)),
@@ -500,9 +505,9 @@
         ),
         in_specs=[
             row_block(cols),
-            row_block(cols),
             row_block(rank),
-            pl.BlockSpec((cols, rank), lambda i: (0, 0)),
+            pl.BlockSpec((rank, cols), lambda i: (0, 0)),
+            pl.BlockSpec((cols // parts, rank), lambda i: (i, 0)),
             pl.BlockSpec((1, rank), lambda i: (0, 0)),
         ],
         out_specs=[
@@ -510,7 +515,7 @@
             row_block(cols),
             pl.BlockSpec((cols // parts, rank), lambda i: (i, 0)),
         ],
-    )(momentum, gradient, basis, factor, norms)
+    )(following, basis, factor_t, factor, norms)
 
 
 def solution(mesh):

time: 112 us -> 115 us (1.027)
  Pallas kernels: 111 us -> 115 us
    pallas_call x1, Pallas kernels: 106 us -> 110 us  [body(): pl.pallas_call(functools.partial(kernel, sizes), out_shape=(jax.ShapeDtyp...]
where the time goes in v2:
time: 115 us
  Pallas kernels  115 us (100%)
    pallas_call x1, Pallas kernels, body(): pl.pallas_call(functools.partial(kernel, sizes), out_shape=(jax.ShapeDtyp...  110 us
    pallas_call x1, Pallas kernels, body(): pl.pallas_call(outputs, grid=(parts,), out_shape=(jax.ShapeDtypeStruct((r...  4.44 us

profile of v2, /device:TPU:1, one launch (start us, length us, event | category | flops | bytes accessed | tf_op | source)
XLA Modules:
  0.0 115.2 jit_solution(12661603634855352257)
XLA Ops:
  0.6 110.1 %shard_map.58 = (f32[512,512]{1,0:T(8,128)}, bf16[512,512]{1,0:T(8,128)(2,1)}, bf16[448,512]{1,0:T(8,128)(2,1)}, bf16[448,512]{1,0:T(8,128)(2,1)}, f32[1,512]{1,0:T(1,128)}) custom-call(bf16[448,512]{1,0:T(8,128)(2,1)} %m_in.1, bf16[448,512]{1,0:T(8,128)(2,1)} %g_in.1, f32[512,512]{1,0:T(8,128)} %r_in.1), custom_call_target="tpu_custom_call" | custom-call | tf_op jit(solution)/shard_map/pallas_call | solution.py:451
  110.7 4.4 %shard_map.59 = (bf16[448,512]{1,0:T(8,128)(2,1)}, f32[448,512]{1,0:T(8,128)}, f32[512,512]{1,0:T(8,128)}) custom-call(bf16[448,512]{1,0:T(8,128)(2,1)} %get-tuple-element.8.mn_in, bf16[448,512]{1,0:T(8,128)(2,1)} %get-tuple-element.9.q_ref, bf16[512,512]{1,0:T(8,128)(2,1)} %get-tuple-element.10.ft_ref, f32[512,512]{1,0:T(8,128)} %get-tuple-element.11.f_ref, ...), custom_call_target="tpu_custom_call" | custom-call | tf_op jit(solution)/shard_map/pallas_call | solution.py:498

commit v3 on v2

--- a/solution.py
+++ b/solution.py
@@ -213,11 +213,14 @@
     m_in, g_in, r_in,
     fac_out, fact_out, qb_out, mn_out, inv_out,
     m_ref, g_ref, r_ref, buft, part, steps, flat, own, ph, pl_,
-    gpart, gwhole, g_c, g_x, g_y, g_own, g_z,
-    hpart, hwhole, h_c, h_x, h_y,
+    ga_part, ga_whole, ga_c, ga_x, ga_y, ga_own, ga_z,
+    gb_part, gb_whole, gb_c, gb_x, gb_y, gb_own, gb_z,
+    ha_part, ha_whole, ha_c, ha_x, ha_y,
+    hb_part, hb_whole, hb_c, hb_x, hb_y,
     work, inv_blk, qb, mn, fac, fact, squares, others,
-    io, zs_send, zs_recv, zg_send, zg_recv, g_send, g_recv, z_send, z_recv,
-    h_send, h_recv, q_send, q_recv,
+    io, zs_send, zs_recv, zg_send, zg_recv,
+    ga_send, ga_recv, az_send, az_recv, gb_send, gb_recv, bz_send, bz_recv,
+    ha_send, ha_recv, hb_send, hb_recv, q_send, q_recv,
 ):
     ny, nx, nc, nz = sizes
     y, x, c, z = (lax.axis_index(a) for a in ("y", "x", "c", "z"))
@@ -281,20 +284,6 @@
             own[...] = jnp.zeros((BLK, rank), F32)
 
     gather = Copies(zg_send, zg_recv)
-
-    def relay(s):
-        for k, (group, at) in enumerate(cuts):
-            for way in range(2):
-                length = hops(way, group)
-                if s > length:
-                    continue
-                if s:
-                    gather.arrived((way, s, k))
-                piece = flat.at[rows_at(ahead(1 - way, s), at)]
-                for u in kids(s, length):
-                    where = {"z": ahead(way, u - s)}
-                    gather.start((way, u, k), lambda a=piece, c=where: (a, a, c))
-
     for k, (group, at) in enumerate(cuts):
         terms = [part[rows_at(z, at)]]
         for way in range(2):
@@ -304,11 +293,27 @@
         total = tree_sum(terms)
         flat[rows_at(z, at)] = total
         own[at : at + 8] = total
-    relay(0)
+        piece = flat.at[rows_at(z, at)]
+        for way in range(2):
+            if hops(way, group):
+                where = {"z": ahead(way, 1)}
+                gather.start((way, 1, k), lambda a=piece, c=where: (a, a, c))
+
+    def relay(t):
+        for k, (group, at) in enumerate(cuts):
+            for way in range(2):
+                length = hops(way, group)
+                if t > length + 1:
+                    continue
+                gather.arrived((way, t - 1, k))
+                if t <= length:
+                    piece = flat.at[rows_at(ahead(1 - way, t - 1), at)]
+                    where = {"z": ahead(way, 1)}
+                    gather.start((way, t, k), lambda a=piece, c=where: (a, a, c))
 
     high, low = split(own[...])
     high_t, low_t = split(jnp.transpose(own[...]))
-    for top in range(2):
+    for top, gpart in enumerate((ga_part, gb_part)):
         first = half * top
         gram = mm3(
             (high_t[first : first + half], low_t[first : first + half]),
@@ -316,44 +321,83 @@
             NN,
         )
         for k in range((rank - first) // BLK):
-            at = top * blocks * half + half * k
-            gpart[at : at + half] = gram[:, BLK * k : BLK * (k + 1)]
-    gsum = PlaneSum(sizes, (y, x, c), gpart, gwhole, g_c, g_x, g_y, g_send, g_recv)
-    hsum = PlaneSum(sizes, (y, x, c), hpart, hwhole, h_c, h_x, h_y, h_send, h_recv)
-    gsum.send_c()
-    gsum.send_x()
-    relay(1)
-    gsum.send_y()
+            gpart[half * k : half * (k + 1)] = gram[:, BLK * k : BLK * (k + 1)]
+    me = (y, x, c)
+    ga = PlaneSum(sizes, me, ga_part, ga_whole, ga_c, ga_x, ga_y, ga_send, ga_recv)
+    gb = PlaneSum(sizes, me, gb_part, gb_whole, gb_c, gb_x, gb_y, gb_send, gb_recv)
+    ha = PlaneSum(sizes, me, ha_part, ha_whole, ha_c, ha_x, ha_y, ha_send, ha_recv)
+    hb = PlaneSum(sizes, me, hb_part, hb_whole, hb_c, hb_x, hb_y, hb_send, hb_recv)
+    across_a = Copies(az_send, az_recv)
+    across_b = Copies(bz_send, bz_recv)
+
+    def send_z(plane, mine, theirs, across):
+        mine[...] = plane.plane_total()
+        for d in range(1, nz):
+            where = {"z": lax.rem(z + d, nz)}
+            across.start(d, lambda d=d, c=where: (mine, theirs.at[d - 1], c))
+
+    def total_z(mine, theirs, across):
+        for d in range(1, nz):
+            across.arrived(d)
+        return tree_sum([mine[...]] + [theirs[d] for d in range(nz - 1)])
+
+    ga.send_c()
+    gb.send_c()
     relay(2)
-    g_own[...] = gsum.plane_total()
-    across = Copies(z_send, z_recv)
-    for d in range(1, nz):
-        where = {"z": lax.rem(z + d, nz)}
-        across.start(d, lambda d=d, c=where: (g_own, g_z.at[d - 1], c))
-    for s in (4, 3, 5, 6):
-        relay(s)
+    ga.send_x()
+    gb.send_x()
+    for t in range(3, 4):
+        if t < longer + 1:
+            relay(t)
+    ga.send_y()
+    gb.send_y()
+    for t in range(4, 6):
+        if t < longer + 1:
+            relay(t)
+    send_z(ga, ga_own, ga_z, across_a)
+    for t in range(6, longer + 1):
+        relay(t)
+    send_z(gb, gb_own, gb_z, across_b)
+    relay(longer + 1)
 
     for k in range(blocks):
         cols = slice(BLK * k, BLK * (k + 1))
         ph[:, cols], pl_[:, cols] = split(flat[0:rows, cols])
-    product = mm(buft[...], ph[...], NN) + mm(buft[...], pl_[...], NN)
+    for side, (plane, hpart) in enumerate(((ha, ha_part), (hb, hb_part))):
+        cols = slice(half * side, half * (side + 1))
+        product = mm(buft[...], ph[:, cols], NN) + mm(buft[...], pl_[:, cols], NN)
+        for k in range(blocks // 2):
+            hpart[rank * k : rank * (k + 1)] = product[:, BLK * k : BLK * (k + 1)]
+        plane.send_c()
+    ha.send_x()
+    hb.send_x()
+    ga.spread_y(total_z(ga_own, ga_z, across_a))
+    gb.spread_y(total_z(gb_own, gb_z, across_b))
+    ha.send_y()
+    ga.spread_x()
+    hb.send_y()
+    gb.spread_x()
+    ga.spread_c()
+    ha.spread_y(ha.plane_total())
+    hb.spread_y(hb.plane_total())
+    ga.finish()
     for k in range(blocks):
-        hpart[rank * k : rank * (k + 1)] = product[:, BLK * k : BLK * (k + 1)]
-    hsum.send_c()
-    hsum.send_x()
-    for d in range(1, nz):
-        across.arrived(d)
-    gsum.spread_y(tree_sum([g_own[...]] + [g_z[d] for d in range(nz - 1)]))
-    hsum.send_y()
-    gsum.spread_x()
-    hsum.spread_y(hsum.plane_total())
-    gsum.spread_c()
-    gsum.finish()
-    for k in range(blocks):
-        work[0:half, BLK * k : BLK * (k + 1)] = gwhole[half * k : half * (k + 1)]
-    for k in range(blocks // 2):
-        at = blocks * half + half * k
-        work[half:rank, half + BLK * k : half + BLK * (k + 1)] = gwhole[at : at + half]
+        work[0:half, BLK * k : BLK * (k + 1)] = ga_whole[half * k : half * (k + 1)]
+
+    def add_lower():
+        gb.finish()
+        for k in range(blocks // 2):
+            work[half:rank, half + BLK * k : half + BLK * (k + 1)] += gb_whole[
+                half * k : half * (k + 1)
+            ]
+
+    def spread_x():
+        ha.spread_x()
+        hb.spread_x()
+
+    def spread_c():
+        ha.spread_c()
+        hb.spread_c()
 
     eye = lax.broadcasted_iota(jnp.int32, (BLK, BLK), 0) == lax.broadcasted_iota(
         jnp.int32, (BLK, BLK), 1
@@ -363,11 +407,13 @@
     def _(at):
         r0 = pl.multiple_of(at * BLK, BLK)
         band = pl.ds(r0, BLK)
+        pl.when(at == 1)(gb.spread_c)
+        pl.when(at == blocks // 2)(add_lower)
         diagonal = [work[pl.ds(pl.multiple_of(r0 + 8 * r, 8), 8), band] for r in range(BLK // 8)]
         for r, tile in enumerate(inverse_factor(diagonal)):
             inv_blk[8 * r : 8 * r + 8, :] = tile
-        pl.when(at == 0)(hsum.spread_x)
-        pl.when(at == 2)(hsum.spread_c)
+        pl.when(at == 1)(spread_x)
+        pl.when(at == 3)(spread_c)
         work[band, band] = eye.astype(F32)
         solved = mm3(split(inv_blk[...]), split(work[band, :]), NN)
         work[band, :] = solved
@@ -382,8 +428,13 @@
 
     block_of = lambda dim: lax.broadcasted_iota(jnp.int32, (rank, rank), dim) // BLK
     inverse = split(jnp.where(block_of(0) >= block_of(1), work[...], 0.0))
-    hsum.finish()
-    whole = jnp.concatenate([hwhole[rank * k : rank * (k + 1)] for k in range(blocks)], axis=1)
+    qb[...] = mm3((ph[...], pl_[...]), inverse, NT).astype(BF16)
+    ha.finish()
+    hb.finish()
+    whole = jnp.concatenate(
+        [h[rank * k : rank * (k + 1)] for h in (ha_whole, hb_whole) for k in range(blocks // 2)],
+        axis=1,
+    )
     factor = mm3(split(whole), inverse, NT)
     squares[...] = jnp.sum(factor * factor, axis=0, keepdims=True)
     totals = Copies(q_send, q_recv)
@@ -392,7 +443,6 @@
         totals.start(d, lambda d=d, c=where: (squares, others.at[d - 1], c))
     fac[...] = factor
     fact[...] = jnp.transpose(factor).astype(BF16)
-    qb[...] = mm3((ph[...], pl_[...]), inverse, NT).astype(BF16)
     stores = [
         pltpu.make_async_copy(src, dst, io.at[k])
         for k, (src, dst) in enumerate(
@@ -411,7 +461,7 @@
     inv_out[...] = 1.0 / jnp.sqrt(total + 1e-06)
     for store in stores:
         store.wait()
-    for copies in (sums, gather, across, totals):
+    for copies in (sums, gather, across_a, across_b, totals):
         copies.sent()
 
 
@@ -431,7 +481,7 @@
     chunk = -(-rows // (8 * nz)) * 8
     longer = nz // 2
     hops = (nz - 1) * (chunk // 8)
-    g_rows, h_rows = 3 * rank, blocks * cols
+    ga_rows, gb_rows, h_rows = 2 * rank, rank, blocks // 2 * cols
     vmem = pltpu.VMEM
 
     def plane(count):
@@ -447,7 +497,10 @@
     def sems(count):
         return [pltpu.SemaphoreType.DMA((count,))] * 2
 
-    piece = g_rows // 2 // nx // ny
+    def crossing(count):
+        piece = count // 2 // nx // ny
+        return [vmem((piece, BLK), F32), vmem((nz - 1, piece, BLK), F32)]
+
     factor, factor_t, basis, following, norms = pl.pallas_call(
         functools.partial(kernel, sizes),
         out_shape=(
@@ -470,9 +523,11 @@
             vmem((BLK, rank), F32),
             vmem((rows, rank), BF16),
             vmem((rows, rank), BF16),
-            *plane(g_rows),
-            vmem((piece, BLK), F32),
-            vmem((nz - 1, piece, BLK), F32),
+            *plane(ga_rows),
+            *crossing(ga_rows),
+            *plane(gb_rows),
+            *crossing(gb_rows),
+            *plane(h_rows),
             *plane(h_rows),
             vmem((rank, rank), F32),
             vmem((BLK, BLK), F32),
@@ -487,6 +542,9 @@
             *sems(hops),
             *sems(PlaneSum.count(sizes)),
             *sems(nz - 1),
+            *sems(PlaneSum.count(sizes)),
+            *sems(nz - 1),
+            *sems(PlaneSum.count(sizes)),
             *sems(PlaneSum.count(sizes)),
             *sems(nz - 1),
         ],

time: 115 us -> 111 us (0.965)
  Pallas kernels: 115 us -> 110 us
    pallas_call x1, Pallas kernels: 110 us -> 106 us  [body(): pl.pallas_call(functools.partial(kernel, sizes), out_shape=(jax.ShapeDtyp...]
where the time goes in v3:
time: 111 us
  Pallas kernels  110 us (99%)
    pallas_call x1, Pallas kernels, body(): pl.pallas_call(functools.partial(kernel, sizes), out_shape=(jax.ShapeDtyp...  106 us
    pallas_call x1, Pallas kernels, body(): pl.pallas_call(outputs, grid=(parts,), out_shape=(jax.ShapeDtypeStruct((r...  4.43 us

profile of v3, /device:TPU:1, one launch (start us, length us, event | category | flops | bytes accessed | tf_op | source)
XLA Modules:
  0.0 111.1 jit_solution(38606611570865568)
XLA Ops:
  0.6 106.0 %shard_map.58 = (f32[512,512]{1,0:T(8,128)}, bf16[512,512]{1,0:T(8,128)(2,1)}, bf16[448,512]{1,0:T(8,128)(2,1)}, bf16[448,512]{1,0:T(8,128)(2,1)}, f32[1,512]{1,0:T(1,128)}) custom-call(bf16[448,512]{1,0:T(8,128)(2,1)} %m_in.1, bf16[448,512]{1,0:T(8,128)(2,1)} %g_in.1, f32[512,512]{1,0:T(8,128)} %r_in.1), custom_call_target="tpu_custom_call" | custom-call | tf_op jit(solution)/shard_map/pallas_call | solution.py:504
  106.7 4.4 %shard_map.59 = (bf16[448,512]{1,0:T(8,128)(2,1)}, f32[448,512]{1,0:T(8,128)}, f32[512,512]{1,0:T(8,128)}) custom-call(bf16[448,512]{1,0:T(8,128)(2,1)} %get-tuple-element.8.mn_in, bf16[448,512]{1,0:T(8,128)(2,1)} %get-tuple-element.9.q_ref, bf16[512,512]{1,0:T(8,128)(2,1)} %get-tuple-element.10.ft_ref, f32[512,512]{1,0:T(8,128)} %get-tuple-element.11.f_ref, ...), custom_call_target="tpu_custom_call" | custom-call | tf_op jit(solution)/shard_map/pallas_call | solution.py:556

commit v4 on v3

--- a/solution.py
+++ b/solution.py
@@ -369,12 +369,12 @@
         for k in range(blocks // 2):
             hpart[rank * k : rank * (k + 1)] = product[:, BLK * k : BLK * (k + 1)]
         plane.send_c()
+    ga.spread_y(total_z(ga_own, ga_z, across_a))
     ha.send_x()
+    gb.spread_y(total_z(gb_own, gb_z, across_b))
     hb.send_x()
-    ga.spread_y(total_z(ga_own, ga_z, across_a))
-    gb.spread_y(total_z(gb_own, gb_z, across_b))
+    ga.spread_x()
     ha.send_y()
-    ga.spread_x()
     hb.send_y()
     gb.spread_x()
     ga.spread_c()

time: 111 us -> 112 us (level)
  no operation moved by 1% of the time
where the time goes in v4:
time: 112 us; the launch traced here: 111 us
  Pallas kernels  111 us (99%)
    pallas_call x1, Pallas kernels, body(): pl.pallas_call(functools.partial(kernel, sizes), out_shape=(jax.ShapeDtyp...  106 us
    pallas_call x1, Pallas kernels, body(): pl.pallas_call(outputs, grid=(parts,), out_shape=(jax.ShapeDtypeStruct((r...  4.43 us

profile of v4, /device:TPU:1, one launch (start us, length us, event | category | flops | bytes accessed | tf_op | source)
XLA Modules:
  0.0 111.4 jit_solution(1723279881419382311)
XLA Ops:
  0.6 106.3 %shard_map.58 = (f32[512,512]{1,0:T(8,128)}, bf16[512,512]{1,0:T(8,128)(2,1)}, bf16[448,512]{1,0:T(8,128)(2,1)}, bf16[448,512]{1,0:T(8,128)(2,1)}, f32[1,512]{1,0:T(1,128)}) custom-call(bf16[448,512]{1,0:T(8,128)(2,1)} %m_in.1, bf16[448,512]{1,0:T(8,128)(2,1)} %g_in.1, f32[512,512]{1,0:T(8,128)} %r_in.1), custom_call_target="tpu_custom_call" | custom-call | tf_op jit(solution)/shard_map/pallas_call | solution.py:504
  107.0 4.4 %shard_map.59 = (bf16[448,512]{1,0:T(8,128)(2,1)}, f32[448,512]{1,0:T(8,128)}, f32[512,512]{1,0:T(8,128)}) custom-call(bf16[448,512]{1,0:T(8,128)(2,1)} %get-tuple-element.8.mn_in, bf16[448,512]{1,0:T(8,128)(2,1)} %get-tuple-element.9.q_ref, bf16[512,512]{1,0:T(8,128)(2,1)} %get-tuple-element.10.ft_ref, f32[512,512]{1,0:T(8,128)} %get-tuple-element.11.f_ref, ...), custom_call_target="tpu_custom_call" | custom-call | tf_op jit(solution)/shard_map/pallas_call | solution.py:556
